TPU v7x, 128 devices: a whole 4x4x4 slice. The times are simulated.
128 devices in a mesh: seq: 16 (over x_hi, y, core), fsdp: 2 (over x_lo), dp: 4 (over z).
Axes of the slice: x: 4 (x_hi: 2, x_lo: 2; x = x_hi * 2 + x_lo), y: 4, z: 4, core: 2. Of those that a mesh axis runs over, the one named last changes fastest.
Arguments:
- queries: bfloat16 [8, 4096, 4096], P(('fsdp', 'dp'), 'seq'), may hold values from -160 to 160
- hidden: bfloat16 [8, 4096, 8192], P(('fsdp', 'dp'), 'seq'), may hold values from -8 to 8
- key_weight: bfloat16 [8192, 512], P('fsdp'), may hold values from -1 to 1
- doc_lengths: int32 [8, 32], P(('fsdp', 'dp')), may hold values from 1 to 256, 4096 in all within a row
- entropy_cot: bfloat16 [8, 4096, 32], P(('fsdp', 'dp'), 'seq'), may hold values from -600 to 600
Outputs:
- entropy: float32 [8, 4096, 32], P(('fsdp', 'dp'), 'seq')
- grad_queries: bfloat16 [8, 4096, 4096], P(('fsdp', 'dp'), 'seq')
- grad_key_weight: bfloat16 [8192, 512], P('fsdp')
Inputs may be any that keep to these rules, and one draw needn't show every extreme that they name: `doc_lengths`: each sequence's 32 documents are packed in order, their lengths sum to 4096, and the longest is exactly 256.
All inputs are finite; a program needn't handle non-finite values.
Results may differ from a plain program's by a relative error of at most 0.0088.
Values may be sent and summed in bfloat16 or wider, within the bound.
No kernel may reach another device: no remote copies, remote signals or barrier semaphores. Data moves between devices by JAX's collectives and lax.ppermute only.
A program may use at most 128 MiB of HBM per device.

v0:
```python
import jax
import jax.numpy as jnp
from jax import lax
from jax.sharding import PartitionSpec as P

QH = 32
KVH = 4
HD = 128


def document_index(lengths, seq_len):
    ends = jnp.cumsum(lengths)
    position = jnp.arange(seq_len, dtype=jnp.int32)
    return jnp.sum((ends[None, :] <= position[:, None]).astype(jnp.int32), axis=1)


def attend(queries, key_rows, cotangent, doc_index, doc_len):
    row_count, key_heads, group_size, head_size = queries.shape
    full_len = key_rows.shape[0]
    block_rows = min(512, row_count)
    window = block_rows + doc_len
    factor = head_size ** (-0.5)
    keys_padded = jnp.concatenate(
        [jnp.zeros((doc_len, key_heads, head_size), key_rows.dtype), key_rows], axis=0
    )
    index_padded = jnp.concatenate([jnp.full((doc_len,), -1, jnp.int32), doc_index], axis=0)

    def one_block(step_index, state_now):
        entropy, grad_query, grad_key = state_now
        row_start = (step_index * block_rows).astype(jnp.int32)
        query_block = lax.dynamic_slice_in_dim(queries, row_start, block_rows, 0)
        weight_block = lax.dynamic_slice_in_dim(cotangent, row_start, block_rows, 0).astype(
            jnp.float32
        )
        key_block = lax.dynamic_slice_in_dim(keys_padded, row_start, window, 0)
        key_docs = lax.dynamic_slice_in_dim(index_padded, row_start, window, 0)
        query_docs = lax.dynamic_slice_in_dim(doc_index, row_start, block_rows, 0)
        query_pos = row_start + jnp.arange(block_rows, dtype=jnp.int32)
        key_pos = row_start - doc_len + jnp.arange(window, dtype=jnp.int32)
        visible = (query_docs[:, None] == key_docs[None, :]) & (
            key_pos[None, :] <= query_pos[:, None]
        )
        scores = (
            jnp.einsum("rkgd,wkd->kgrw", query_block, key_block, preferred_element_type=jnp.float32)
            * factor
        )
        scores = jnp.where(visible, scores, -1e30)
        row_max = jnp.max(scores, axis=-1, keepdims=True)
        powers = jnp.exp(scores - row_max)
        denominator = jnp.sum(powers, axis=-1, keepdims=True)
        probability = powers / denominator
        mean_score = jnp.sum(jnp.where(visible, probability * scores, 0.0), axis=-1, keepdims=True)
        block_entropy = (row_max + jnp.log(denominator) - mean_score)[..., 0]
        row_weight = jnp.transpose(weight_block, (1, 2, 0))[..., None]
        slope = jnp.where(visible, row_weight * probability * (mean_score - scores), 0.0).astype(
            jnp.bfloat16
        )
        query_part = (
            jnp.einsum("kgrw,wkd->rkgd", slope, key_block, preferred_element_type=jnp.float32)
            * factor
        )
        key_part = (
            jnp.einsum("kgrw,rkgd->wkd", slope, query_block, preferred_element_type=jnp.float32)
            * factor
        )
        entropy = lax.dynamic_update_slice_in_dim(
            entropy, jnp.transpose(block_entropy, (2, 0, 1)), row_start, 0
        )
        grad_query = lax.dynamic_update_slice_in_dim(grad_query, query_part, row_start, 0)
        previous = lax.dynamic_slice_in_dim(grad_key, row_start, window, 0)
        grad_key = lax.dynamic_update_slice_in_dim(grad_key, previous + key_part, row_start, 0)
        return (entropy, grad_query, grad_key)

    initial = (
        jnp.zeros((row_count, key_heads, group_size), jnp.float32),
        jnp.zeros((row_count, key_heads, group_size, head_size), jnp.float32),
        jnp.zeros((full_len + doc_len, key_heads, head_size), jnp.float32),
    )
    entropy, grad_query, grad_key = lax.fori_loop(0, row_count // block_rows, one_block, initial)
    return (entropy, grad_query, grad_key[doc_len:])


def shards(queries, hidden, key_weight, doc_lengths, entropy_cot):
    tokens = hidden[0]
    local_rows = tokens.shape[0]
    seq_parts = lax.axis_size("seq")
    seq_len = local_rows * seq_parts
    group_size = QH // KVH
    doc_index = document_index(doc_lengths[0], seq_len)
    columns = tokens
    key_local = jnp.dot(
        columns,
        lax.all_gather(key_weight, "fsdp", axis=0, tiled=True),
        preferred_element_type=jnp.float32,
    ).astype(jnp.bfloat16)
    query_local = queries[0]
    cot_local = entropy_cot[0]
    share = QH // seq_parts
    outgoing = jnp.broadcast_to(
        key_local.reshape(local_rows, KVH, 1, HD), (local_rows, KVH, group_size, HD)
    )
    outgoing = outgoing.reshape(local_rows, KVH * group_size * HD)
    query_heads, key_heads_seq, cot_heads = (
        lax.all_to_all(query_local, "seq", split_axis=1, concat_axis=0, tiled=True),
        lax.all_to_all(outgoing, "seq", split_axis=1, concat_axis=0, tiled=True),
        lax.all_to_all(cot_local, "seq", split_axis=1, concat_axis=0, tiled=True),
    )
    key_count = key_heads_seq.shape[1] // HD
    entropy, grad_query, grad_key = attend(
        query_heads.reshape(seq_len, key_count, share // key_count, HD),
        key_heads_seq.reshape(seq_len, key_count, HD),
        cot_heads.reshape(seq_len, key_count, share // key_count),
        doc_index,
        local_rows,
    )
    grad_local, key_grad_local, entropy_local = (
        lax.all_to_all(
            grad_query.reshape(seq_len, share * HD), "seq", split_axis=0, concat_axis=1, tiled=True
        ),
        lax.all_to_all(
            grad_key.reshape(seq_len, key_count * HD),
            "seq",
            split_axis=0,
            concat_axis=1,
            tiled=True,
        ),
        lax.all_to_all(
            entropy.reshape(seq_len, share), "seq", split_axis=0, concat_axis=1, tiled=True
        ),
    )
    key_grad = jnp.sum(key_grad_local.reshape(local_rows, KVH, -1, HD), axis=2).reshape(
        local_rows, KVH * HD
    )
    key_grad_low = key_grad.astype(jnp.bfloat16)
    columns = tokens
    term_rows = lax.psum_scatter(
        lax.dot_general(
            columns, key_grad_low, (((0,), (0,)), ((), ())), preferred_element_type=jnp.float32
        ),
        "fsdp",
        scatter_dimension=0,
        tiled=True,
    )
    summed = lax.psum(term_rows, ("seq", "dp"))
    norm_factor = (seq_len * lax.axis_size("fsdp") * lax.axis_size("dp")) ** (-0.5)
    weight_grad = (summed * norm_factor).astype(jnp.bfloat16)
    return (
        entropy_local.reshape(1, local_rows, QH),
        grad_local.astype(jnp.bfloat16).reshape(1, local_rows, QH * HD),
        weight_grad,
    )


def solution(mesh):
    return jax.shard_map(
        shards,
        mesh=mesh,
        in_specs=(
            P(("fsdp", "dp"), "seq", None),
            P(("fsdp", "dp"), "seq", None),
            P("fsdp", None),
            P(("fsdp", "dp"), None),
            P(("fsdp", "dp"), "seq", None),
        ),
        out_specs=(P(("fsdp", "dp"), "seq", None), P(("fsdp", "dp"), "seq", None), P("fsdp", None)),
        check_vma=False,
    )
```

profile of v0, /device:TPU:0, one launch (start us, length us, event | category | flops | bytes accessed | tf_op | source)
XLA Modules:
  0.0 1256.6 jit_solution(18081824443787886025)
XLA Ops:
  11.2 7.1 all-to-all-start.1
  18.3 114.7 %all-gather.2.cloned.1.call-done = bf16[8192,512]{1,0:T(8,128)(2,1)} async-done(((bf16[4096,512]{1,0:T(8,128)(2,1)}), bf16[8192,512]{1,0:T(8,128)(2,1)}) %all-gather.2.cloned.1.call-update) | async-done | bytes 8388624 | tf_op jit(solution)/shard_map/all_gather | solution.py:93
  133.0 7.0 fusion.41
  141.7 8.3 all-to-all-start
  150.9 28.5 %all-to-all-done = bf16[256,16,256]{0,2,1:T(8,128)(2,1)} async-done(((bf16[256,16,256]{0,2,1:T(8,128)(2,1)}), bf16[256,16,256]{0,2,1:T(8,128)(2,1)}, u32[]{:S(2)}, u32[]{:S(2)}) %all-to-all-start) | async-done | bytes 2097184 | tf_op jit(solution)/shard_map/all_to_all | solution.py:105
  179.3 6.3 all-to-all-start.2
  186.0 2.5 copy.84
  188.5 4.2 reshape.222
  192.7 4.1 copy.82
  196.8 2.9 reshape.221
  204.4 88.0 %while.19 = (s32[]{:T(128)}, f32[4096,2,1]{0,1,2:T(2,128)}, bf16[4096,2,1,128]{0,3,1,2:T(8,128)(2,1)S(1)}, f32[4352,2,128]{0,2,1:T(8,128)}, s32[4096]{0:T(1024)S...) while((s32[]{:T(128)}, f32[4096,2,1]{0,1,2:T(2,128)}, ...), condition=%wide.region_6.7_spmd, body=%wide.region_2.6_spmd.sunk | while | flops 630850816 | bytes 21601552 | solution.py:79
  211.7 3.7 fusion.61
  222.7 3.6 fusion.61
  233.7 3.7 fusion.61
  244.7 3.7 fusion.61
  255.7 3.7 fusion.61
  266.7 3.7 fusion.61
  277.7 3.7 fusion.61
  288.7 3.7 fusion.61
  292.4 2.5 slice.3
  299.1 58.8 %all_to_all.93 = f32[16,256,256]{1,2,0:T(8,128)} all-to-all(f32[16,256,256]{1,2,0:T(8,128)S(1)} %copy.90), channel_id=1, replica_groups=mesh['seq'=16,'fsdp'=2,'dp'=4] {'seq'}, dimensions={0} | all-to-all | bytes 8388608 | tf_op jit(solution)/shard_map/all_to_all | solution.py:120
  357.9 2.5 reduce_sum.41
  360.4 10.3 convolution_bitcast_fusion
  370.7 189.8 %reduce-scatter.2.cloned.1.call-done = f32[4096,512]{0,1:T(8,128)} async-done(((f32[8192,512]{0,1:T(8,128)}), f32[4096,512]{0,1:T(8,128)}) %reduce-scatter.2.cloned.1.call-update) | async-done | bytes 8388624 | tf_op jit(solution)/shard_map/reduce_scatter | solution.py:136
  560.6 6.5 all-to-all-start.3
  569.1 4.3 copy.98
  574.7 5.9 all-to-all-start.4
  581.2 29.5 %all-to-all-done.4 = bf16[16,256,256]{2,1,0:T(8,128)(2,1)S(1)} async-done(((bf16[16,256,256]{2,1,0:T(8,128)(2,1)}), bf16[16,256,256]{2,1,0:T(8,128)(2,1)S(1)}, u32[]{:S(2)}, u32[]{:S(2)}) %all-to-all-start.4) | async-done | bytes 2097184 | tf_op jit(solution)/shard_map/all_to_all | solution.py:117
  613.0 4.1 copy.91
  617.1 620.1 %all-reduce.4.cloned.1.call-done = f32[4096,512]{0,1:T(8,128)} async-done(((f32[4096,512]{0,1:T(8,128)}), f32[4096,512]{0,1:T(8,128)}) %all-reduce.4.cloned.1.call-update) | async-done | bytes 8388624 | tf_op jit(solution)/shard_map/psum | solution.py:144
  1237.3 6.4 multiply_convert_fusion
  1243.6 6.4 copy.92
  (121 shorter events, 80.7 us)
Async XLA Ops:
  7.2 1.6 copy-start
  7.2 125.8 %all-gather.2.cloned.1.call-start = ((), (), s32[]{:S(2)}) async-start(), calls=%async_computation.7 | async-start | bytes 12582912 | tf_op jit(solution)/shard_map/all_gather | solution.py:93
  11.2 128.9 %all-to-all-start.1 = ((bf16[256,16,256]{0,2,1:T(8,128)(2,1)}), bf16[256,16,256]{0,2,1:T(8,128)(2,1)S(1)}, u32[]{:S(2)}, u32[]{:S(2)}) async-start(bf16[256,16,256]{0,2,1:T(8,128)(2,1)} %bitcast.144), calls=%async_computation.1 | async-start | bytes 4194304 | tf_op jit(solution)/shard_map/all_to_all | solution.py:104
  140.1 9.9 copy-start.2
  140.1 10.1 copy-start.1
  141.7 37.6 %all-to-all-start = ((bf16[256,16,256]{0,2,1:T(8,128)(2,1)}), bf16[256,16,256]{0,2,1:T(8,128)(2,1)}, u32[]{:S(2)}, u32[]{:S(2)}) async-start(bf16[256,16,256]{0,2,1:T(8,128)(2,1)} %bitcast.145), calls=%async_computation | async-start | bytes 4194304 | tf_op jit(solution)/shard_map/all_to_all | solution.py:105
  179.3 21.9 %all-to-all-start.2 = ((bf16[256,16,2]{0,2,1:T(2,128)(2,1)}), bf16[256,16,2]{0,2,1:T(2,128)(2,1)S(1)}, u32[]{:S(2)}, u32[]{:S(2)}) async-start(bf16[256,16,2]{0,2,1:T(2,128)(2,1)} %all_to_all.76), calls=%async_computation.2 | async-start | bytes 32768 | tf_op jit(solution)/shard_map/all_to_all | solution.py:106
  185.6 374.9 %reduce-scatter.2.cloned.1.call-start = ((), (), s32[]{:S(2)}) async-start(), calls=%async_computation.8 | async-start | bytes 25165824 | tf_op jit(solution)/shard_map/reduce_scatter | solution.py:136
  370.7 866.6 %all-reduce.4.cloned.1.call-start = ((), (), s32[]{:S(2)}) async-start(), calls=%async_computation.9 | async-start | bytes 16777216 | tf_op jit(solution)/shard_map/psum | solution.py:144
  560.6 14.1 %all-to-all-start.3 = ((f32[16,256,2]{1,2,0:T(2,128)}), f32[16,256,2]{1,2,0:T(2,128)S(1)}, u32[]{:S(2)}, u32[]{:S(2)}) async-start(f32[16,256,2]{1,2,0:T(2,128)} %bitcast.20), calls=%async_computation.3 | async-start | bytes 65536 | tf_op jit(solution)/shard_map/all_to_all | solution.py:127
  574.7 36.0 %all-to-all-start.4 = ((bf16[16,256,256]{2,1,0:T(8,128)(2,1)}), bf16[16,256,256]{2,1,0:T(8,128)(2,1)S(1)}, u32[]{:S(2)}, u32[]{:S(2)}) async-start(bf16[16,256,256]{2,1,0:T(8,128)(2,1)} %copy.98), calls=%async_computation.4 | async-start | bytes 4194304 | tf_op jit(solution)/shard_map/all_to_all | solution.py:117
Sparse Core Ops, SparseCore 0:
  9.7 123.2 all-gather.1
  370.8 189.6 reduce-scatter.1
  563.2 674.0 all-reduce.3
where the time goes:
time: 1260 us
  waiting for transfers between devices  985 us (78%)
  matrix products  81.7 us (6%)
  blocking collectives  58.8 us (5%)
  local copies, waits for them, and re-layouts  51.6 us (4%)
  starting transfers between devices  34.4 us (3%)
  other arithmetic  31.4 us (2%)
  between operations  13.9 us (1%)
    psum x1, waiting for transfers between devices, shards(): summed = lax.psum(term_rows, ('seq', 'dp'))  620 us
    reduce_scatter x1, waiting for transfers between devices, shards(): lax.psum_scatter(lax.dot_general(columns, key_grad_low, (((0,), (0,)), ((...  190 us
    all_gather x1, waiting for transfers between devices, shards(): lax.all_gather(key_weight, 'fsdp', axis=0, tiled=True)  115 us
    all_to_all x1, blocking collectives, shards(): lax.all_to_all(grad_key.reshape(seq_len, key_count * HD), 'seq', split_ax...  58.8 us
    all_to_all x1, waiting for transfers between devices, shards(): lax.all_to_all(grad_query.reshape(seq_len, share * HD), 'seq', split_axis...  29.5 us
    dot_general x8, matrix products, one_block(): jnp.einsum('kgrw,rkgd->wkd', slope, query_block, preferred_element_type=j...  29.3 us
    all_to_all x1, waiting for transfers between devices, shards(): lax.all_to_all(outgoing, 'seq', split_axis=1, concat_axis=0, tiled=True)  28.5 us
  transfers between devices with their start and end apart: 8, of which 6 were waited for; matrix products, arithmetic and copies ran while one was open for 3% of the time, Pallas kernels for 0%

commit v1 on v0

--- a/solution.py
+++ b/solution.py
@@ -141,7 +141,9 @@
         scatter_dimension=0,
         tiled=True,
     )
-    summed = lax.psum(term_rows, ("seq", "dp"))
+    summed = term_rows
+    for mesh_axis in ("seq", "dp"):
+        summed = lax.psum(summed, mesh_axis)
     norm_factor = (seq_len * lax.axis_size("fsdp") * lax.axis_size("dp")) ** (-0.5)
     weight_grad = (summed * norm_factor).astype(jnp.bfloat16)
     return (

time: 1260 us -> 913 us (0.72)
  waiting for transfers between devices: 985 us -> 639 us
    psum x1 -> x2, waiting for transfers between devices: 620 us -> 276 us  [shards(): summed = lax.psum(summed, mesh_axis)]
  transfers between devices with their start and end apart: 8 -> 9, of which waited for: 6 -> 7; matrix products, arithmetic and copies ran while one was open for 3% -> 4% of each run, Pallas kernels for 0% -> 0%
where the time goes in v1:
time: 913 us; the launch traced here: 911 us
  waiting for transfers between devices  639 us (70%)
  matrix products  81.7 us (9%)
  blocking collectives  58.8 us (6%)
  local copies, waits for them, and re-layouts  51.7 us (6%)
  starting transfers between devices  33.9 us (4%)
  other arithmetic  31.3 us (3%)
  between operations  13.9 us (2%)
    psum x2, waiting for transfers between devices, shards(): summed = lax.psum(summed, mesh_axis)  276 us
    reduce_scatter x1, waiting for transfers between devices, shards(): lax.psum_scatter(lax.dot_general(columns, key_grad_low, (((0,), (0,)), ((...  190 us
    all_gather x1, waiting for transfers between devices, shards(): lax.all_gather(key_weight, 'fsdp', axis=0, tiled=True)  115 us
    all_to_all x1, blocking collectives, shards(): lax.all_to_all(grad_key.reshape(seq_len, key_count * HD), 'seq', split_ax...  58.8 us
    dot_general x8, matrix products, one_block(): jnp.einsum('kgrw,rkgd->wkd', slope, query_block, preferred_element_type=j...  29.3 us
    all_to_all x1, waiting for transfers between devices, shards(): lax.all_to_all(grad_query.reshape(seq_len, share * HD), 'seq', split_axis...  28.7 us
    all_to_all x1, waiting for transfers between devices, shards(): lax.all_to_all(outgoing, 'seq', split_axis=1, concat_axis=0, tiled=True)  28.5 us
    dot_general x8, matrix products, one_block(): jnp.einsum('kgrw,wkd->rkgd', slope, key_block, preferred_element_type=jnp...  19.7 us
  transfers between devices with their start and end apart: 9, of which 7 were waited for; matrix products, arithmetic and copies ran while one was open for 4% of the time, Pallas kernels for 0%

profile of v1, /device:TPU:0, one launch (start us, length us, event | category | flops | bytes accessed | tf_op | source)
XLA Modules:
  0.0 910.6 jit_solution(6381320456182857525)
XLA Ops:
  11.2 7.1 all-to-all-start.1
  18.3 114.7 %all-gather.2.cloned.1.call-done = bf16[8192,512]{1,0:T(8,128)(2,1)} async-done(((bf16[4096,512]{1,0:T(8,128)(2,1)}), bf16[8192,512]{1,0:T(8,128)(2,1)}) %all-gather.2.cloned.1.call-update) | async-done | bytes 8388624 | tf_op jit(solution)/shard_map/all_gather | solution.py:93
  133.0 7.0 fusion.41
  141.7 8.3 all-to-all-start
  150.9 28.5 %all-to-all-done = bf16[256,16,256]{0,2,1:T(8,128)(2,1)} async-done(((bf16[256,16,256]{0,2,1:T(8,128)(2,1)}), bf16[256,16,256]{0,2,1:T(8,128)(2,1)}, u32[]{:S(2)}, u32[]{:S(2)}) %all-to-all-start) | async-done | bytes 2097184 | tf_op jit(solution)/shard_map/all_to_all | solution.py:105
  179.3 6.3 all-to-all-start.2
  186.0 2.5 copy.84
  188.5 4.2 reshape.222
  192.7 4.1 copy.82
  196.8 2.9 reshape.221
  204.4 88.0 %while.19 = (s32[]{:T(128)}, f32[4096,2,1]{0,1,2:T(2,128)}, bf16[4096,2,1,128]{0,3,1,2:T(8,128)(2,1)S(1)}, f32[4352,2,128]{0,2,1:T(8,128)}, s32[4096]{0:T(1024)S...) while((s32[]{:T(128)}, f32[4096,2,1]{0,1,2:T(2,128)}, ...), condition=%wide.region_6.7_spmd, body=%wide.region_2.6_spmd.sunk | while | flops 630850816 | bytes 21601552 | solution.py:79
  211.7 3.7 fusion.61
  222.7 3.6 fusion.61
  233.7 3.7 fusion.61
  244.7 3.7 fusion.61
  255.7 3.7 fusion.61
  266.7 3.7 fusion.61
  277.7 3.7 fusion.61
  288.7 3.7 fusion.61
  299.1 58.8 %all_to_all.93 = f32[16,256,256]{1,2,0:T(8,128)} all-to-all(f32[16,256,256]{1,2,0:T(8,128)S(1)} %copy.90), channel_id=1, replica_groups=mesh['seq'=16,'fsdp'=2,'dp'=4] {'seq'}, dimensions={0} | all-to-all | bytes 8388608 | tf_op jit(solution)/shard_map/all_to_all | solution.py:120
  357.9 2.5 reduce_sum.41
  360.4 10.3 %convolution_bitcast_fusion = f32[8192,512]{0,1:T(8,128)} fusion(bf16[256,512]{0,1:T(8,128)(2,1)S(1)} %bitcast.150, bf16[1,256,8192]{2,1,0:T(8,128)(2,1)} %param.8), kind=kOutput, calls=%fused_computation.33 | convolution fusion | flops 2147483648 | bytes 21233664 | tf_op jit(solution)/shard_map/dot_general | solution.py:137
  370.7 189.8 %reduce-scatter.2.cloned.1.call-done = f32[4096,512]{0,1:T(8,128)} async-done(((f32[8192,512]{0,1:T(8,128)}), f32[4096,512]{0,1:T(8,128)}) %reduce-scatter.2.cloned.1.call-update) | async-done | bytes 8388624 | tf_op jit(solution)/shard_map/reduce_scatter | solution.py:136
  560.6 167.4 %all-reduce.5.cloned.1.call-done = f32[4096,512]{0,1:T(8,128)} async-done(((f32[4096,512]{0,1:T(8,128)}), f32[4096,512]{0,1:T(8,128)}) %all-reduce.5.cloned.1.call-update) | async-done | bytes 8388624 | tf_op jit(solution)/shard_map/psum | solution.py:146
  728.1 5.8 all-to-all-start.3
  735.9 4.3 copy.98
  741.5 6.0 all-to-all-start.4
  748.2 28.7 %all-to-all-done.4 = bf16[16,256,256]{2,1,0:T(8,128)(2,1)S(1)} async-done(((bf16[16,256,256]{2,1,0:T(8,128)(2,1)}), bf16[16,256,256]{2,1,0:T(8,128)(2,1)S(1)}, u32[]{:S(2)}, u32[]{:S(2)}) %all-to-all-start.4) | async-done | bytes 2097184 | tf_op jit(solution)/shard_map/all_to_all | solution.py:117
  779.2 4.1 copy.91
  783.3 108.1 %all-reduce.7.cloned.1.call-done = f32[4096,512]{0,1:T(8,128)} async-done(((f32[4096,512]{0,1:T(8,128)}), f32[4096,512]{0,1:T(8,128)}) %all-reduce.7.cloned.1.call-update) | async-done | bytes 8388624 | tf_op jit(solution)/shard_map/psum | solution.py:146
  891.3 6.3 multiply_convert_fusion
  897.7 6.4 copy.92
  (124 shorter events, 83.2 us)
Async XLA Ops:
  7.2 1.6 copy-start
  7.2 125.8 %all-gather.2.cloned.1.call-start = ((), (), s32[]{:S(2)}) async-start(), calls=%async_computation.7 | async-start | bytes 12582912 | tf_op jit(solution)/shard_map/all_gather | solution.py:93
  11.2 128.9 %all-to-all-start.1 = ((bf16[256,16,256]{0,2,1:T(8,128)(2,1)}), bf16[256,16,256]{0,2,1:T(8,128)(2,1)S(1)}, u32[]{:S(2)}, u32[]{:S(2)}) async-start(bf16[256,16,256]{0,2,1:T(8,128)(2,1)} %bitcast.144), calls=%async_computation.1 | async-start | bytes 4194304 | tf_op jit(solution)/shard_map/all_to_all | solution.py:104
  140.1 9.9 %copy-start.2 = (s32[1,32]{1,0:T(1,128)S(1)}, s32[1,32]{1,0:T(1,128)}, u32[]{:S(2)}) copy-start(s32[1,32]{1,0:T(1,128)} %param.10) | copy-start | bytes 388
  140.1 10.1 %copy-start.1 = (bf16[1,256,32]{1,2,0:T(8,128)(2,1)S(1)}, bf16[1,256,32]{1,2,0:T(8,128)(2,1)}, u32[]{:S(2)}) copy-start(bf16[1,256,32]{1,2,0:T(8,128)(2,1)} %param.11) | copy-start | bytes 49156
  141.7 37.6 %all-to-all-start = ((bf16[256,16,256]{0,2,1:T(8,128)(2,1)}), bf16[256,16,256]{0,2,1:T(8,128)(2,1)}, u32[]{:S(2)}, u32[]{:S(2)}) async-start(bf16[256,16,256]{0,2,1:T(8,128)(2,1)} %bitcast.145), calls=%async_computation | async-start | bytes 4194304 | tf_op jit(solution)/shard_map/all_to_all | solution.py:105
  179.3 21.9 %all-to-all-start.2 = ((bf16[256,16,2]{0,2,1:T(2,128)(2,1)}), bf16[256,16,2]{0,2,1:T(2,128)(2,1)S(1)}, u32[]{:S(2)}, u32[]{:S(2)}) async-start(bf16[256,16,2]{0,2,1:T(2,128)(2,1)} %all_to_all.76), calls=%async_computation.2 | async-start | bytes 32768 | tf_op jit(solution)/shard_map/all_to_all | solution.py:106
  185.6 374.9 %reduce-scatter.2.cloned.1.call-start = ((), (), s32[]{:S(2)}) async-start(), calls=%async_computation.8 | async-start | bytes 25165824 | tf_op jit(solution)/shard_map/reduce_scatter | solution.py:136
  370.7 357.4 %all-reduce.5.cloned.1.call-start = ((), (), s32[]{:S(2)}) async-start(), calls=%async_computation.9 | async-start | bytes 16777216 | tf_op jit(solution)/shard_map/psum | solution.py:146
  560.6 330.8 %all-reduce.7.cloned.1.call-start = ((), (), s32[]{:S(2)}) async-start(), calls=%async_computation.10 | async-start | bytes 16777216 | tf_op jit(solution)/shard_map/psum | solution.py:146
  728.1 13.4 %all-to-all-start.3 = ((f32[16,256,2]{1,2,0:T(2,128)}), f32[16,256,2]{1,2,0:T(2,128)S(1)}, u32[]{:S(2)}, u32[]{:S(2)}) async-start(f32[16,256,2]{1,2,0:T(2,128)} %bitcast.20), calls=%async_computation.3 | async-start | bytes 65536 | tf_op jit(solution)/shard_map/all_to_all | solution.py:127
  741.5 35.3 %all-to-all-start.4 = ((bf16[16,256,256]{2,1,0:T(8,128)(2,1)}), bf16[16,256,256]{2,1,0:T(8,128)(2,1)S(1)}, u32[]{:S(2)}, u32[]{:S(2)}) async-start(bf16[16,256,256]{2,1,0:T(8,128)(2,1)} %copy.98), calls=%async_computation.4 | async-start | bytes 4194304 | tf_op jit(solution)/shard_map/all_to_all | solution.py:117
Sparse Core Ops, SparseCore 0:
  9.7 123.2 all-gather.1
  370.8 189.6 reduce-scatter.1
  563.2 164.7 all-reduce.4
  730.5 160.7 all-reduce.6
